TPU v7x, 32 devices: a whole 2x2x4 slice. The times are simulated.
32 devices in a mesh: row: 4 (over z), col: 4 (over x, core), layer: 2 (over y).
Axes of the slice: x: 2, y: 2, z: 4, core: 2. Of those that a mesh axis runs over, the one named last changes fastest.
Arguments:
- left_blocks: float32 [4, 2, 4, 4, 128, 128], P('row', 'layer', 'col'), may hold values from -1.2 to 1.2
- right_blocks: float32 [2, 4, 4, 8, 128, 128], P('layer', 'row', 'col'), may hold values from -1.2 to 1.2
- pair_stacks: int32 [4, 4, 2, 4, 3, 32], P('row', 'col', 'layer'), may hold values from 0 to 32, as said below
Outputs:
- product_window: float32 [4, 4, 32, 128, 128], P('row', 'col', 'layer')
Inputs may be any that keep to these rules, and one draw needn't show every extreme that they name: `pair_stacks`: entry 0 of a list holds left slots below 4, entry 1 right slots below 8, entry 2 product blocks below 32; the live triples stand first, every other slot holds (0, 0, 32); some list is live in all 32 slots.
All inputs are finite; a program needn't handle non-finite values.
Results may differ from a plain program's by a relative error of at most 0.0003.
Values sent between devices are 32-bit elements; how exact they have to be, the bound alone decides.
A program may use at most 64 MiB of HBM per device.

v0:
```python
import jax
import jax.numpy as jnp
from jax import lax
from jax.sharding import PartitionSpec as P

OUT_TILE = 32


def multiply(running, left_piece, right_piece, left_slot, right_slot, out_slot):
    first_blocks = jnp.take(left_piece, left_slot, axis=0)
    second_blocks = jnp.take(right_piece, right_slot, axis=0)
    products = jnp.einsum(
        "qxy,qyz->qxz",
        first_blocks,
        second_blocks,
        precision=lax.Precision.HIGHEST,
        preferred_element_type=jnp.float32,
    )
    return running.at[out_slot].add(products, mode="drop")


def piece_term(accumulated, left_piece, right_piece, triples):
    left_slot = triples[0]
    right_slot = triples[1]
    out_slot = triples[2]
    return multiply(accumulated, left_piece, right_piece, left_slot, right_slot, out_slot)


def body(left_blocks, right_blocks, pair_stacks):
    left_local = left_blocks[0, 0]
    right_local = right_blocks[0, :, 0]
    stacks = pair_stacks[0, 0, 0]
    block_width = left_local.shape[-1]
    initial = jnp.zeros((OUT_TILE, block_width, block_width), jnp.float32)
    right_whole = lax.all_gather(right_local, "row", axis=0, tiled=True)
    pieces = lax.all_gather(left_local, "col", axis=0, tiled=True)

    def visit(position, running):
        left_piece = lax.dynamic_index_in_dim(pieces, position, 0, keepdims=False)
        right_piece = lax.dynamic_index_in_dim(right_whole, position, 0, keepdims=False)
        triples = lax.dynamic_index_in_dim(stacks, position, 0, keepdims=False)
        return piece_term(running, left_piece, right_piece, triples)

    accumulated = lax.fori_loop(0, pieces.shape[0], visit, initial)
    reduced = lax.psum_scatter(accumulated, "layer", scatter_dimension=0, tiled=True)
    return reduced[None, None]


def solution(mesh):
    placed = (
        P("row", "layer", "col", None, None, None),
        P("layer", "row", "col", None, None, None),
        P("row", "col", "layer", None, None, None),
    )
    return jax.shard_map(
        body,
        mesh=mesh,
        in_specs=placed,
        out_specs=P("row", "col", "layer", None, None),
        check_vma=False,
    )
```

profile of v0, /device:TPU:0, one launch (start us, length us, event | category | flops | bytes accessed | tf_op | source)
XLA Modules:
  0.0 182.1 jit_solution(6074862939140767157)
XLA Ops:
  8.7 19.6 %all-gather.5.cloned.1.call-done = f32[4,1,1,4,128,128]{5,4,3,2,1,0:T(8,128)} async-done(((f32[1,1,1,4,128,128]{5,4,3,2,1,0:T(8,128)}), f32[4,1,1,4,128,128]{5,4,3,2,1,0:T(8,128)}) %all-gather.5.cloned.1.call-update) | async-done | bytes 1048592 | tf_op jit(solution)/shard_map/all_gather | solution.py:36
  28.4 47.5 %all-gather.7.cloned.1.call-done = f32[4,1,1,8,128,128]{5,4,3,2,1,0:T(8,128)} async-done(((f32[1,1,1,8,128,128]{5,4,3,2,1,0:T(8,128)}), f32[4,1,1,8,128,128]{5,4,3,2,1,0:T(8,128)}) %all-gather.7.cloned.1.call-update) | async-done | bytes 2097168 | tf_op jit(solution)/shard_map/all_gather | solution.py:35
  75.9 1.6 broadcast_in_dim.43
  77.5 66.5 %while.13 = (s32[]{:T(128)}, f32[32,128,128]{2,1,0:T(8,128)}, s32[4,3,32]{2,1,0:T(4,128)S(1)}, f32[4,4,128,128]{3,2,1,0:T(8,128)}, f32[4,8,128,128]{3,2,1,0:T(8,128)}, /*index=5*/s32[]{:T(128)}) while((s32[]{:T(128)}, f32[32,128,128]{2,1,0:T(8,128)}, s32[4,3,32]{2,1,0:T(4,128)S(1)}, f32[4,4,128,128]{3,2,1,0:T(8,128)}, ...), condition=%wide.region_2.3_spmd, body=%wide.region_0.2_spmd.sunk | while | flops 806881984 | bytes 22555224 | solution.py:44
  78.5 1.1 dynamic-slice_bitcast_fusion.4
  79.6 2.0 %gather_fusion = f32[32,128,128]{2,1,0:T(8,128)} fusion(f32[8,128,128]{2,1,0:T(8,128)S(1)} %dynamic-slice_bitcast_fusion.4, s32[1024]{0:T(1024)S(1)} %get-tuple-element.158), kind=kCustom, calls=%fused_computation.1.clone.1 | custom fusion | bytes 4194432 | tf_op jit(solution)/shard_map/while/body/eval_jaxpr/jit(_take)/gather | solution.py:11
  81.6 2.0 %gather_fusion.1 = f32[32,128,128]{2,1,0:T(8,128)} fusion(f32[4,128,128]{2,1,0:T(8,128)S(1)} %dynamic-slice_bitcast_fusion.5, s32[1024]{0:T(1024)S(1)} %get-tuple-element.159), kind=kCustom, calls=%fused_computation.clone.1 | custom fusion | bytes 4194432 | tf_op jit(solution)/shard_map/while/body/eval_jaxpr/jit(_take)/gather | solution.py:10
  83.6 4.6 %fusion.17 = f32[32,128,128]{2,1,0:T(8,128)S(1)} fusion(f32[32,128,128]{2,1,0:T(8,128)} %gather_fusion, f32[32,128,128]{2,1,0:T(8,128)} %gather_fusion.1, pred[32]{0:T(512)(128)(4,1)S(1)} %get-tuple-element.160, pred[32]{0:T(512)(128)(4,1)S(1)} %get-tuple-element.161), kind=kOutput, calls=%fused_computation.3.clone.1 | convolution fusion | flops 806354944 | bytes 6291520 | tf_op jit(solution)/shard_map/while/body/eval_jaxpr/qxy,qyz->qxz/dot_general | solution.py:12
  88.2 5.9 %scatter_fusion = f32[32,128,128]{2,1,0:T(8,128)} fusion(f32[32,128,128]{2,1,0:T(8,128)} %get-tuple-element.169, s32[32]{0:T(128)S(1)} %get-tuple-element.155, f32[32,128,128]{2,1,0:T(8,128)S(1)} %fusion.17), kind=kCustom, calls=%fused_computation.2.clone.1 | custom fusion | flops 524288 | bytes 6291584 | tf_op jit(solution)/shard_map/while/body/eval_jaxpr/scatter-add | solution.py:19
  95.2 1.1 dynamic-slice_bitcast_fusion.4
  96.3 2.0 %gather_fusion = f32[32,128,128]{2,1,0:T(8,128)} fusion(f32[8,128,128]{2,1,0:T(8,128)S(1)} %dynamic-slice_bitcast_fusion.4, s32[1024]{0:T(1024)S(1)} %get-tuple-element.158), kind=kCustom, calls=%fused_computation.1.clone.1 | custom fusion | bytes 4194432 | tf_op jit(solution)/shard_map/while/body/eval_jaxpr/jit(_take)/gather | solution.py:11
  98.3 2.0 %gather_fusion.1 = f32[32,128,128]{2,1,0:T(8,128)} fusion(f32[4,128,128]{2,1,0:T(8,128)S(1)} %dynamic-slice_bitcast_fusion.5, s32[1024]{0:T(1024)S(1)} %get-tuple-element.159), kind=kCustom, calls=%fused_computation.clone.1 | custom fusion | bytes 4194432 | tf_op jit(solution)/shard_map/while/body/eval_jaxpr/jit(_take)/gather | solution.py:10
  100.3 4.6 %fusion.17 = f32[32,128,128]{2,1,0:T(8,128)S(1)} fusion(f32[32,128,128]{2,1,0:T(8,128)} %gather_fusion, f32[32,128,128]{2,1,0:T(8,128)} %gather_fusion.1, pred[32]{0:T(512)(128)(4,1)S(1)} %get-tuple-element.160, pred[32]{0:T(512)(128)(4,1)S(1)} %get-tuple-element.161), kind=kOutput, calls=%fused_computation.3.clone.1 | convolution fusion | flops 806354944 | bytes 6291520 | tf_op jit(solution)/shard_map/while/body/eval_jaxpr/qxy,qyz->qxz/dot_general | solution.py:12
  104.8 5.9 %scatter_fusion = f32[32,128,128]{2,1,0:T(8,128)} fusion(f32[32,128,128]{2,1,0:T(8,128)} %get-tuple-element.169, s32[32]{0:T(128)S(1)} %get-tuple-element.155, f32[32,128,128]{2,1,0:T(8,128)S(1)} %fusion.17), kind=kCustom, calls=%fused_computation.2.clone.1 | custom fusion | flops 524288 | bytes 6291584 | tf_op jit(solution)/shard_map/while/body/eval_jaxpr/scatter-add | solution.py:19
  111.8 1.1 dynamic-slice_bitcast_fusion.4
  112.9 2.0 %gather_fusion = f32[32,128,128]{2,1,0:T(8,128)} fusion(f32[8,128,128]{2,1,0:T(8,128)S(1)} %dynamic-slice_bitcast_fusion.4, s32[1024]{0:T(1024)S(1)} %get-tuple-element.158), kind=kCustom, calls=%fused_computation.1.clone.1 | custom fusion | bytes 4194432 | tf_op jit(solution)/shard_map/while/body/eval_jaxpr/jit(_take)/gather | solution.py:11
  114.9 2.0 %gather_fusion.1 = f32[32,128,128]{2,1,0:T(8,128)} fusion(f32[4,128,128]{2,1,0:T(8,128)S(1)} %dynamic-slice_bitcast_fusion.5, s32[1024]{0:T(1024)S(1)} %get-tuple-element.159), kind=kCustom, calls=%fused_computation.clone.1 | custom fusion | bytes 4194432 | tf_op jit(solution)/shard_map/while/body/eval_jaxpr/jit(_take)/gather | solution.py:10
  116.9 4.6 %fusion.17 = f32[32,128,128]{2,1,0:T(8,128)S(1)} fusion(f32[32,128,128]{2,1,0:T(8,128)} %gather_fusion, f32[32,128,128]{2,1,0:T(8,128)} %gather_fusion.1, pred[32]{0:T(512)(128)(4,1)S(1)} %get-tuple-element.160, pred[32]{0:T(512)(128)(4,1)S(1)} %get-tuple-element.161), kind=kOutput, calls=%fused_computation.3.clone.1 | convolution fusion | flops 806354944 | bytes 6291520 | tf_op jit(solution)/shard_map/while/body/eval_jaxpr/qxy,qyz->qxz/dot_general | solution.py:12
  121.4 5.9 %scatter_fusion = f32[32,128,128]{2,1,0:T(8,128)} fusion(f32[32,128,128]{2,1,0:T(8,128)} %get-tuple-element.169, s32[32]{0:T(128)S(1)} %get-tuple-element.155, f32[32,128,128]{2,1,0:T(8,128)S(1)} %fusion.17), kind=kCustom, calls=%fused_computation.2.clone.1 | custom fusion | flops 524288 | bytes 6291584 | tf_op jit(solution)/shard_map/while/body/eval_jaxpr/scatter-add | solution.py:19
  129.5 2.0 %gather_fusion = f32[32,128,128]{2,1,0:T(8,128)} fusion(f32[8,128,128]{2,1,0:T(8,128)S(1)} %dynamic-slice_bitcast_fusion.4, s32[1024]{0:T(1024)S(1)} %get-tuple-element.158), kind=kCustom, calls=%fused_computation.1.clone.1 | custom fusion | bytes 4194432 | tf_op jit(solution)/shard_map/while/body/eval_jaxpr/jit(_take)/gather | solution.py:11
  131.5 2.0 %gather_fusion.1 = f32[32,128,128]{2,1,0:T(8,128)} fusion(f32[4,128,128]{2,1,0:T(8,128)S(1)} %dynamic-slice_bitcast_fusion.5, s32[1024]{0:T(1024)S(1)} %get-tuple-element.159), kind=kCustom, calls=%fused_computation.clone.1 | custom fusion | bytes 4194432 | tf_op jit(solution)/shard_map/while/body/eval_jaxpr/jit(_take)/gather | solution.py:10
  133.5 4.6 %fusion.17 = f32[32,128,128]{2,1,0:T(8,128)S(1)} fusion(f32[32,128,128]{2,1,0:T(8,128)} %gather_fusion, f32[32,128,128]{2,1,0:T(8,128)} %gather_fusion.1, pred[32]{0:T(512)(128)(4,1)S(1)} %get-tuple-element.160, pred[32]{0:T(512)(128)(4,1)S(1)} %get-tuple-element.161), kind=kOutput, calls=%fused_computation.3.clone.1 | convolution fusion | flops 806354944 | bytes 6291520 | tf_op jit(solution)/shard_map/while/body/eval_jaxpr/qxy,qyz->qxz/dot_general | solution.py:12
  138.1 5.9 %scatter_fusion = f32[32,128,128]{2,1,0:T(8,128)} fusion(f32[32,128,128]{2,1,0:T(8,128)} %get-tuple-element.169, s32[32]{0:T(128)S(1)} %get-tuple-element.155, f32[32,128,128]{2,1,0:T(8,128)S(1)} %fusion.17), kind=kCustom, calls=%fused_computation.2.clone.1 | custom fusion | flops 524288 | bytes 6291584 | tf_op jit(solution)/shard_map/while/body/eval_jaxpr/scatter-add | solution.py:19
  144.0 31.5 %reduce-scatter.2.cloned.1.call-done = f32[16,128,128]{2,1,0:T(8,128)} async-done(((f32[32,128,128]{2,1,0:T(8,128)}), f32[16,128,128]{2,1,0:T(8,128)}) %reduce-scatter.2.cloned.1.call-update) | async-done | bytes 1048592 | tf_op jit(solution)/shard_map/reduce_scatter | solution.py:45
  (28 shorter events, 7.3 us)
Async XLA Ops:
  6.5 21.8 %all-gather.5.cloned.1.call-start = ((), (), s32[]{:S(2)}) async-start(), calls=%async_computation.2 | async-start | bytes 1310720 | tf_op jit(solution)/shard_map/all_gather | solution.py:36
  7.3 68.7 %all-gather.7.cloned.1.call-start = ((), (), s32[]{:S(2)}) async-start(), calls=%async_computation.3 | async-start | bytes 2621440 | tf_op jit(solution)/shard_map/all_gather | solution.py:35
  8.0 167.5 %reduce-scatter.2.cloned.1.call-start = ((), (), s32[]{:S(2)}) async-start(), calls=%async_computation.1 | async-start | bytes 3145728 | tf_op jit(solution)/shard_map/reduce_scatter | solution.py:45
Sparse Core Ops, SparseCore 0:
  8.9 19.4 all-gather.4
  29.9 45.9 all-gather.6
  144.1 31.3 reduce-scatter.1
where the time goes:
time: 183 us; the launch traced here: 182 us
  waiting for transfers between devices  100 us (55%)
  local copies, waits for them, and re-layouts  26.5 us (14%)
  other arithmetic  23.7 us (13%)
  matrix products  18.2 us (10%)
  between operations  13.1 us (7%)
    all_gather x1, waiting for transfers between devices, body(): right_whole = lax.all_gather(right_local, 'row', axis=0, tiled=True)  47.5 us
    reduce_scatter x1, waiting for transfers between devices, body(): lax.psum_scatter(accumulated, 'layer', scatter_dimension=0, tiled=True)  31.5 us
    scatter-add x4, other arithmetic, multiply(): return running.at[out_slot].add(products, mode='drop')  23.7 us
    all_gather x1, waiting for transfers between devices, body(): pieces = lax.all_gather(left_local, 'col', axis=0, tiled=True)  19.6 us
    dot_general x4, matrix products, multiply(): jnp.einsum('qxy,qyz->qxz', first_blocks, second_blocks, precision=lax.Pre...  18.2 us
    gather x4, local copies, waits for them, and re-layouts, multiply(): first_blocks = jnp.take(left_piece, left_slot, axis=0)  8.03 us
    gather x4, local copies, waits for them, and re-layouts, multiply(): second_blocks = jnp.take(right_piece, right_slot, axis=0)  7.96 us
    squeeze x4, local copies, waits for them, and re-layouts, visit(): lax.dynamic_index_in_dim(right_whole, position, 0, keepdims=False)  4.33 us
  transfers between devices with their start and end apart: 3, of which 3 were waited for; matrix products, arithmetic and copies ran while one was open for 0% of the time, Pallas kernels for 0%

commit v1 on v0

--- a/solution.py
+++ b/solution.py
@@ -4,6 +4,16 @@
 from jax.sharding import PartitionSpec as P
 
 OUT_TILE = 32
+
+
+def gather_by_hops(x, mesh_axis, d):
+    peers = lax.axis_size(mesh_axis)
+    held, shards = (x, [x])
+    for _ in range(peers - 1):
+        held = lax.ppermute(held, mesh_axis, [(i, (i + 1) % peers) for i in range(peers)])
+        shards.insert(0, held)
+    line = jnp.concatenate(shards, axis=d)
+    return jnp.roll(line, (lax.axis_index(mesh_axis) + 1) * x.shape[d], axis=d)
 
 
 def multiply(running, left_piece, right_piece, left_slot, right_slot, out_slot):
@@ -32,7 +42,7 @@
     stacks = pair_stacks[0, 0, 0]
     block_width = left_local.shape[-1]
     initial = jnp.zeros((OUT_TILE, block_width, block_width), jnp.float32)
-    right_whole = lax.all_gather(right_local, "row", axis=0, tiled=True)
+    right_whole = gather_by_hops(right_local, "row", 0)
     pieces = lax.all_gather(left_local, "col", axis=0, tiled=True)
 
     def visit(position, running):

time: 183 us -> 166 us (0.907)
  waiting for transfers between devices: 100 us -> 77.4 us
  starting transfers between devices: 0.08 us -> 3.07 us
    all_gather x1 -> x0, waiting for transfers between devices: 47.5 us -> none  [body(): right_whole = lax.all_gather(right_local, 'row', axis=0, tiled=True)]
    ppermute x0 -> x3, waiting for transfers between devices: none -> 42.3 us  [gather_by_hops(): lax.ppermute(held, mesh_axis, [(i, (i + 1) % peers) for i in range(peers)])]
    all_gather x1, waiting for transfers between devices: 19.6 us -> 2.36 us  [body(): pieces = lax.all_gather(left_local, 'col', axis=0, tiled=True)]
    ppermute x0 -> x3, starting transfers between devices: none -> 3.03 us  [gather_by_hops(): lax.ppermute(held, mesh_axis, [(i, (i + 1) % peers) for i in range(peers)])]
  transfers between devices with their start and end apart: 3 -> 5, of which waited for: 3 -> 5; matrix products, arithmetic and copies ran while one was open for 0% -> 2% of each run, Pallas kernels for 0% -> 0%
where the time goes in v1:
time: 166 us; the launch traced here: 165 us
  waiting for transfers between devices  77.4 us (47%)
  local copies, waits for them, and re-layouts  28.3 us (17%)
  other arithmetic  23.8 us (14%)
  matrix products  18.2 us (11%)
  between operations  13.5 us (8%)
  starting transfers between devices  3.07 us (2%)
    ppermute x3, waiting for transfers between devices, gather_by_hops(): lax.ppermute(held, mesh_axis, [(i, (i + 1) % peers) for i in range(peers)])  42.3 us
    reduce_scatter x1, waiting for transfers between devices, body(): lax.psum_scatter(accumulated, 'layer', scatter_dimension=0, tiled=True)  32.7 us
    scatter-add x4, other arithmetic, multiply(): return running.at[out_slot].add(products, mode='drop')  23.8 us
    dot_general x4, matrix products, multiply(): jnp.einsum('qxy,qyz->qxz', first_blocks, second_blocks, precision=lax.Pre...  18.2 us
    gather x4, local copies, waits for them, and re-layouts, multiply(): first_blocks = jnp.take(left_piece, left_slot, axis=0)  8.02 us
    gather x4, local copies, waits for them, and re-layouts, multiply(): second_blocks = jnp.take(right_piece, right_slot, axis=0)  7.94 us
    squeeze x4, local copies, waits for them, and re-layouts, visit(): lax.dynamic_index_in_dim(right_whole, position, 0, keepdims=False)  4.33 us
    squeeze x4, local copies, waits for them, and re-layouts, visit(): left_piece = lax.dynamic_index_in_dim(pieces, position, 0, keepdims=False)  3.87 us
  transfers between devices with their start and end apart: 5, of which 5 were waited for; matrix products, arithmetic and copies ran while one was open for 2% of the time, Pallas kernels for 0%

profile of v1, /device:TPU:0, one launch (start us, length us, event | category | flops | bytes accessed | tf_op | source)
XLA Modules:
  0.0 164.5 jit_solution(3467298692775811031)
XLA Ops:
  6.5 3.0 %collective-permute-start = (f32[1,8,128,128]{3,2,1,0:T(8,128)}, f32[1,8,128,128]{3,2,1,0:T(8,128)S(1)}, u32[]{:S(2)}, u32[]{:S(2)}) collective-permute-start(f32[1,8,128,128]{3,2,1,0:T(8,128)} %bitcast.38), channel_id=1, source_target_pairs={{0,8},{8,16},{16,24},{24,0},{1,9},{9,17},{17,25},{25,1},{2,10},{10... | collective-permute-start | bytes 1572872 | tf_op jit(solution)/shard_map/ppermute | solution.py:13
  9.6 14.2 %collective-permute-done = f32[1,8,128,128]{3,2,1,0:T(8,128)S(1)} collective-permute-done((f32[1,8,128,128]{3,2,1,0:T(8,128)}, f32[1,8,128,128]{3,2,1,0:T(8,128)S(1)}, u32[]{:S(2)}, u32[]{:S(2)}) %collective-permute-start) | collective-permute-done | bytes 524320 | tf_op jit(solution)/shard_map/ppermute | solution.py:13
  23.8 14.9 %collective-permute-done.1 = f32[1,8,128,128]{3,2,1,0:T(8,128)S(1)} collective-permute-done((f32[1,8,128,128]{3,2,1,0:T(8,128)S(1)}, f32[1,8,128,128]{3,2,1,0:T(8,128)S(1)}, u32[]{:S(2)}, u32[]{:S(2)}) %collective-permute-start.1) | collective-permute-done | bytes 524320 | tf_op jit(solution)/shard_map/ppermute | solution.py:13
  39.5 13.2 %collective-permute-done.2 = f32[1,8,128,128]{3,2,1,0:T(8,128)S(1)} collective-permute-done((f32[1,8,128,128]{3,2,1,0:T(8,128)S(1)}, f32[1,8,128,128]{3,2,1,0:T(8,128)S(1)}, u32[]{:S(2)}, u32[]{:S(2)}) %collective-permute-start.2) | collective-permute-done | bytes 524320 | tf_op jit(solution)/shard_map/ppermute | solution.py:13
  54.5 2.4 %all-gather.3.cloned.1.call-done = f32[4,1,1,4,128,128]{5,4,3,2,1,0:T(8,128)} async-done(((f32[1,1,1,4,128,128]{5,4,3,2,1,0:T(8,128)}), f32[4,1,1,4,128,128]{5,4,3,2,1,0:T(8,128)}) %all-gather.3.cloned.1.call-update) | async-done | bytes 1048592 | tf_op jit(solution)/shard_map/all_gather | solution.py:46
  56.9 1.6 broadcast_in_dim.43
  58.5 66.5 %while.13 = (s32[]{:T(128)}, f32[32,128,128]{2,1,0:T(8,128)}, s32[4,3,32]{2,1,0:T(4,128)S(1)}, f32[4,4,128,128]{3,2,1,0:T(8,128)}, f32[4,8,128,128]{3,2,1,0:T(8,128)}, /*index=5*/s32[]{:T(128)}) while((s32[]{:T(128)}, f32[32,128,128]{2,1,0:T(8,128)}, s32[4,3,32]{2,1,0:T(4,128)S(1)}, f32[4,4,128,128]{3,2,1,0:T(8,128)}, ...), condition=%wide.region_2.3_spmd, body=%wide.region_0.2_spmd.sunk | while | flops 806881984 | bytes 22555216 | solution.py:54
  59.6 2.0 %gather_fusion = f32[32,128,128]{2,1,0:T(8,128)} fusion(f32[8,128,128]{2,1,0:T(8,128)S(1)} %dynamic-slice_bitcast_fusion.4, s32[1024]{0:T(1024)S(1)} %get-tuple-element.158), kind=kCustom, calls=%fused_computation.1.clone.1 | custom fusion | bytes 4194432 | tf_op jit(solution)/shard_map/while/body/eval_jaxpr/jit(_take)/gather | solution.py:21
  62.6 2.0 %gather_fusion.1 = f32[32,128,128]{2,1,0:T(8,128)} fusion(f32[4,128,128]{2,1,0:T(8,128)S(1)} %dynamic-slice_bitcast_fusion.5, s32[1024]{0:T(1024)S(1)} %get-tuple-element.159), kind=kCustom, calls=%fused_computation.clone.1 | custom fusion | bytes 4194432 | tf_op jit(solution)/shard_map/while/body/eval_jaxpr/jit(_take)/gather | solution.py:20
  64.6 4.6 %fusion.17 = f32[32,128,128]{2,1,0:T(8,128)S(1)} fusion(f32[32,128,128]{2,1,0:T(8,128)} %gather_fusion, f32[32,128,128]{2,1,0:T(8,128)} %gather_fusion.1, pred[32]{0:T(512)(128)(4,1)S(1)} %get-tuple-element.160, pred[32]{0:T(512)(128)(4,1)S(1)} %get-tuple-element.161), kind=kOutput, calls=%fused_computation.3.clone.1 | convolution fusion | flops 806354944 | bytes 6291520 | tf_op jit(solution)/shard_map/while/body/eval_jaxpr/qxy,qyz->qxz/dot_general | solution.py:22
  69.1 6.0 %scatter_fusion = f32[32,128,128]{2,1,0:T(8,128)} fusion(f32[32,128,128]{2,1,0:T(8,128)} %get-tuple-element.169, s32[32]{0:T(128)S(1)} %get-tuple-element.155, f32[32,128,128]{2,1,0:T(8,128)S(1)} %fusion.17), kind=kCustom, calls=%fused_computation.2.clone.1 | custom fusion | flops 524288 | bytes 6291584 | tf_op jit(solution)/shard_map/while/body/eval_jaxpr/scatter-add | solution.py:29
  76.2 2.0 %gather_fusion = f32[32,128,128]{2,1,0:T(8,128)} fusion(f32[8,128,128]{2,1,0:T(8,128)S(1)} %dynamic-slice_bitcast_fusion.4, s32[1024]{0:T(1024)S(1)} %get-tuple-element.158), kind=kCustom, calls=%fused_computation.1.clone.1 | custom fusion | bytes 4194432 | tf_op jit(solution)/shard_map/while/body/eval_jaxpr/jit(_take)/gather | solution.py:21
  79.2 2.0 %gather_fusion.1 = f32[32,128,128]{2,1,0:T(8,128)} fusion(f32[4,128,128]{2,1,0:T(8,128)S(1)} %dynamic-slice_bitcast_fusion.5, s32[1024]{0:T(1024)S(1)} %get-tuple-element.159), kind=kCustom, calls=%fused_computation.clone.1 | custom fusion | bytes 4194432 | tf_op jit(solution)/shard_map/while/body/eval_jaxpr/jit(_take)/gather | solution.py:20
  81.2 4.6 %fusion.17 = f32[32,128,128]{2,1,0:T(8,128)S(1)} fusion(f32[32,128,128]{2,1,0:T(8,128)} %gather_fusion, f32[32,128,128]{2,1,0:T(8,128)} %gather_fusion.1, pred[32]{0:T(512)(128)(4,1)S(1)} %get-tuple-element.160, pred[32]{0:T(512)(128)(4,1)S(1)} %get-tuple-element.161), kind=kOutput, calls=%fused_computation.3.clone.1 | convolution fusion | flops 806354944 | bytes 6291520 | tf_op jit(solution)/shard_map/while/body/eval_jaxpr/qxy,qyz->qxz/dot_general | solution.py:22
  85.8 5.9 %scatter_fusion = f32[32,128,128]{2,1,0:T(8,128)} fusion(f32[32,128,128]{2,1,0:T(8,128)} %get-tuple-element.169, s32[32]{0:T(128)S(1)} %get-tuple-element.155, f32[32,128,128]{2,1,0:T(8,128)S(1)} %fusion.17), kind=kCustom, calls=%fused_computation.2.clone.1 | custom fusion | flops 524288 | bytes 6291584 | tf_op jit(solution)/shard_map/while/body/eval_jaxpr/scatter-add | solution.py:29
  92.9 2.0 %gather_fusion = f32[32,128,128]{2,1,0:T(8,128)} fusion(f32[8,128,128]{2,1,0:T(8,128)S(1)} %dynamic-slice_bitcast_fusion.4, s32[1024]{0:T(1024)S(1)} %get-tuple-element.158), kind=kCustom, calls=%fused_computation.1.clone.1 | custom fusion | bytes 4194432 | tf_op jit(solution)/shard_map/while/body/eval_jaxpr/jit(_take)/gather | solution.py:21
  95.8 2.0 %gather_fusion.1 = f32[32,128,128]{2,1,0:T(8,128)} fusion(f32[4,128,128]{2,1,0:T(8,128)S(1)} %dynamic-slice_bitcast_fusion.5, s32[1024]{0:T(1024)S(1)} %get-tuple-element.159), kind=kCustom, calls=%fused_computation.clone.1 | custom fusion | bytes 4194432 | tf_op jit(solution)/shard_map/while/body/eval_jaxpr/jit(_take)/gather | solution.py:20
  97.8 4.6 %fusion.17 = f32[32,128,128]{2,1,0:T(8,128)S(1)} fusion(f32[32,128,128]{2,1,0:T(8,128)} %gather_fusion, f32[32,128,128]{2,1,0:T(8,128)} %gather_fusion.1, pred[32]{0:T(512)(128)(4,1)S(1)} %get-tuple-element.160, pred[32]{0:T(512)(128)(4,1)S(1)} %get-tuple-element.161), kind=kOutput, calls=%fused_computation.3.clone.1 | convolution fusion | flops 806354944 | bytes 6291520 | tf_op jit(solution)/shard_map/while/body/eval_jaxpr/qxy,qyz->qxz/dot_general | solution.py:22
  102.4 5.9 %scatter_fusion = f32[32,128,128]{2,1,0:T(8,128)} fusion(f32[32,128,128]{2,1,0:T(8,128)} %get-tuple-element.169, s32[32]{0:T(128)S(1)} %get-tuple-element.155, f32[32,128,128]{2,1,0:T(8,128)S(1)} %fusion.17), kind=kCustom, calls=%fused_computation.2.clone.1 | custom fusion | flops 524288 | bytes 6291584 | tf_op jit(solution)/shard_map/while/body/eval_jaxpr/scatter-add | solution.py:29
  109.5 2.0 %gather_fusion = f32[32,128,128]{2,1,0:T(8,128)} fusion(f32[8,128,128]{2,1,0:T(8,128)S(1)} %dynamic-slice_bitcast_fusion.4, s32[1024]{0:T(1024)S(1)} %get-tuple-element.158), kind=kCustom, calls=%fused_computation.1.clone.1 | custom fusion | bytes 4194432 | tf_op jit(solution)/shard_map/while/body/eval_jaxpr/jit(_take)/gather | solution.py:21
  112.4 2.0 %gather_fusion.1 = f32[32,128,128]{2,1,0:T(8,128)} fusion(f32[4,128,128]{2,1,0:T(8,128)S(1)} %dynamic-slice_bitcast_fusion.5, s32[1024]{0:T(1024)S(1)} %get-tuple-element.159), kind=kCustom, calls=%fused_computation.clone.1 | custom fusion | bytes 4194432 | tf_op jit(solution)/shard_map/while/body/eval_jaxpr/jit(_take)/gather | solution.py:20
  114.5 4.6 %fusion.17 = f32[32,128,128]{2,1,0:T(8,128)S(1)} fusion(f32[32,128,128]{2,1,0:T(8,128)} %gather_fusion, f32[32,128,128]{2,1,0:T(8,128)} %gather_fusion.1, pred[32]{0:T(512)(128)(4,1)S(1)} %get-tuple-element.160, pred[32]{0:T(512)(128)(4,1)S(1)} %get-tuple-element.161), kind=kOutput, calls=%fused_computation.3.clone.1 | convolution fusion | flops 806354944 | bytes 6291520 | tf_op jit(solution)/shard_map/while/body/eval_jaxpr/qxy,qyz->qxz/dot_general | solution.py:22
  119.0 5.9 %scatter_fusion = f32[32,128,128]{2,1,0:T(8,128)} fusion(f32[32,128,128]{2,1,0:T(8,128)} %get-tuple-element.169, s32[32]{0:T(128)S(1)} %get-tuple-element.155, f32[32,128,128]{2,1,0:T(8,128)S(1)} %fusion.17), kind=kCustom, calls=%fused_computation.2.clone.1 | custom fusion | flops 524288 | bytes 6291584 | tf_op jit(solution)/shard_map/while/body/eval_jaxpr/scatter-add | solution.py:29
  125.0 32.7 %reduce-scatter.2.cloned.1.call-done = f32[16,128,128]{2,1,0:T(8,128)} async-done(((f32[32,128,128]{2,1,0:T(8,128)}), f32[16,128,128]{2,1,0:T(8,128)}) %reduce-scatter.2.cloned.1.call-update) | async-done | bytes 1048592 | tf_op jit(solution)/shard_map/reduce_scatter | solution.py:55
  (42 shorter events, 10.9 us)
Async XLA Ops:
  6.5 46.3 %copy-start = (f32[1,1,1,8,128,128]{5,4,3,2,1,0:T(8,128)S(1)}, f32[1,1,1,8,128,128]{5,4,3,2,1,0:T(8,128)}, u32[]{:S(2)}) copy-start(f32[1,1,1,8,128,128]{5,4,3,2,1,0:T(8,128)} %param.6) | copy-start | bytes 1572868
  6.5 50.4 %all-gather.3.cloned.1.call-start = ((), (), s32[]{:S(2)}) async-start(), calls=%async_computation.2 | async-start | bytes 1310720 | tf_op jit(solution)/shard_map/all_gather | solution.py:46
  6.5 17.2 %collective-permute-start = (f32[1,8,128,128]{3,2,1,0:T(8,128)}, f32[1,8,128,128]{3,2,1,0:T(8,128)S(1)}, u32[]{:S(2)}, u32[]{:S(2)}) collective-permute-start(f32[1,8,128,128]{3,2,1,0:T(8,128)} %bitcast.38), channel_id=1, source_target_pairs={{0,8},{8,16},{16,24},{24,0},{1,9},{9,17},{17,25},{25,1},{2,10},{10... | collective-permute-start | bytes 1572872 | tf_op jit(solution)/shard_map/ppermute | solution.py:13
  23.8 14.9 %collective-permute-start.1 = (f32[1,8,128,128]{3,2,1,0:T(8,128)S(1)}, f32[1,8,128,128]{3,2,1,0:T(8,128)S(1)}, u32[]{:S(2)}, u32[]{:S(2)}) collective-permute-start(f32[1,8,128,128]{3,2,1,0:T(8,128)S(1)} %collective-permute-done), channel_id=1, source_target_pairs={{0,8},{8,16},{16,24},{24,0},{1,9},{9,17},{17,25},{25,1},{2,10},{10... | collective-permute-start | bytes 1572872 | tf_op jit(solution)/shard_map/ppermute | solution.py:13
  38.7 14.0 %collective-permute-start.2 = (f32[1,8,128,128]{3,2,1,0:T(8,128)S(1)}, f32[1,8,128,128]{3,2,1,0:T(8,128)S(1)}, u32[]{:S(2)}, u32[]{:S(2)}) collective-permute-start(f32[1,8,128,128]{3,2,1,0:T(8,128)S(1)} %collective-permute-done.1), channel_id=1, source_target_pairs={{0,8},{8,16},{16,24},{24,0},{1,9},{9,17},{17,25},{25,1},{2,10},{10... | collective-permute-start | bytes 1572872 | tf_op jit(solution)/shard_map/ppermute | solution.py:13
  38.7 119.0 %reduce-scatter.2.cloned.1.call-start = ((), (), s32[]{:S(2)}) async-start(), calls=%async_computation.1 | async-start | bytes 3145728 | tf_op jit(solution)/shard_map/reduce_scatter | solution.py:55
Sparse Core Ops, SparseCore 0:
  38.8 18.0 all-gather.2
  125.1 32.5 reduce-scatter.1
